TPU v7x, 32 devices: a whole 2x2x4 slice. The times are simulated.
32 devices in a mesh: dp: 8 (over z, y), mp: 4 (over x, core).
Axes of the slice: x: 2, y: 2, z: 4, core: 2. Of those that a mesh axis runs over, the one named last changes fastest.
Arguments:
- tokens: bfloat16 [8192, 768], P('dp'), may hold values from -6 to 6
- seg_counts: int32 [16], replicated, may hold values from 1 to 16, 64 in all
- seg_order: int32 [64], replicated, may hold values from 0 to 63, each once
- seg_qkv: bfloat16 [768, 3, 768], P(None, None, 'mp'), may hold values from -0.21875 to 0.21875
- seg_qv_bias: float32 [2, 768], P(None, 'mp'), may hold values from -1.75 to 1.75
- seg_out: bfloat16 [768, 768], P('mp'), may hold values from -0.875 to 0.875
- seg_up: bfloat16 [768, 3072], P(None, 'mp'), may hold values from -0.21875 to 0.21875
- seg_up_bias: float32 [3072], P('mp'), may hold values from -1.75 to 1.75
- seg_down: bfloat16 [3072, 768], P('mp'), may hold values from -0.109375 to 0.109375
- seg_gains: float32 [2, 768], replicated, may hold values from 0.5 to 1.5
- seg_shifts: float32 [4, 768], replicated, may hold values from -1.75 to 1.75
- cls_qkv: bfloat16 [768, 3, 768], P(None, None, 'mp'), may hold values from -0.21875 to 0.21875
- cls_qv_bias: float32 [2, 768], P(None, 'mp'), may hold values from -1.75 to 1.75
- cls_out: bfloat16 [768, 768], P('mp'), may hold values from -0.875 to 0.875
- cls_up: bfloat16 [768, 3072], P(None, 'mp'), may hold values from -0.21875 to 0.21875
- cls_up_bias: float32 [3072], P('mp'), may hold values from -1.75 to 1.75
- cls_down: bfloat16 [3072, 768], P('mp'), may hold values from -0.109375 to 0.109375
- cls_gains: float32 [2, 768], replicated, may hold values from 0.5 to 1.5
- cls_shifts: float32 [4, 768], replicated, may hold values from -1.75 to 1.75
- pos_table: bfloat16 [64, 768], replicated, may hold values from -3 to 3
- cotangent: bfloat16 [8192, 768], P('dp'), may hold values from -6 to 6
Outputs:
- layer_out: bfloat16 [8192, 768], P('dp')
- tokens_grad: float32 [8192, 768], P('dp')
- seg_qkv_grad: float32 [768, 3, 768], P(None, None, 'mp')
- seg_qv_bias_grad: float32 [2, 768], P(None, 'mp')
- seg_out_grad: float32 [768, 768], P('mp')
- seg_up_grad: float32 [768, 3072], P(None, 'mp')
- seg_up_bias_grad: float32 [3072], P('mp')
- seg_down_grad: float32 [3072, 768], P('mp')
- seg_gains_grad: float32 [2, 768], replicated
- seg_shifts_grad: float32 [4, 768], replicated
- cls_qkv_grad: float32 [768, 3, 768], P(None, None, 'mp')
- cls_qv_bias_grad: float32 [2, 768], P(None, 'mp')
- cls_out_grad: float32 [768, 768], P('mp')
- cls_up_grad: float32 [768, 3072], P(None, 'mp')
- cls_up_bias_grad: float32 [3072], P('mp')
- cls_down_grad: float32 [3072, 768], P('mp')
- cls_gains_grad: float32 [2, 768], replicated
- cls_shifts_grad: float32 [4, 768], replicated
- pos_table_grad: float32 [64, 768], replicated
Inputs may be any that keep to these rules, and one draw needn't show every extreme that they name: `seg_counts`: the counts sum to 64; the largest is exactly 16. `seg_order`: every segment number appears once.
All inputs are finite; a program needn't handle non-finite values.
Results may differ from a plain program's by a relative error of at most 0.02.
Values may be sent and summed in bfloat16 or wider, within the bound.
No kernel may reach another device: no remote copies, remote signals or barrier semaphores. Data moves between devices by JAX's collectives and lax.ppermute only.
A program may use at most 128 MiB of HBM per device.

v0:
```python
import jax
import jax.numpy as jnp
from jax import lax
from jax.sharding import PartitionSpec as P

HEAD = 64
SEG = 128


EPSILON = 1e-05


def layout(seg_counts, seg_order):
    slot_total = seg_order.shape[0]
    doc_ends = jnp.cumsum(seg_counts)
    doc_starts = doc_ends - seg_counts
    longest = jnp.argmax(seg_counts)
    doc_index = jnp.arange(seg_counts.shape[0], dtype=jnp.int32)
    chosen = doc_index == longest
    lead_seg = jnp.sum(jnp.where(chosen, doc_starts, 0))
    trail_seg = jnp.sum(jnp.where(chosen, doc_ends, 0)) - 1
    slot_index = jnp.arange(slot_total, dtype=jnp.int32)
    lead_slot = jnp.argmax(seg_order == lead_seg)
    slot_seg = jnp.where(
        slot_index == 0, lead_seg, jnp.where(slot_index == lead_slot, seg_order[0], seg_order)
    )
    trail_slot = jnp.argmax(slot_seg == trail_seg)
    slot_seg = jnp.where(
        slot_index == slot_total - 1,
        trail_seg,
        jnp.where(slot_index == trail_slot, slot_seg[slot_total - 1], slot_seg),
    )
    seg_owner = jnp.sum((slot_seg[:, None] >= doc_ends[None, :]).astype(jnp.int32), axis=1)
    seg_start = jnp.sum(
        jnp.where(seg_owner[:, None] == doc_index[None, :], doc_starts[None, :], 0), axis=1
    )
    seg_place = slot_seg - seg_start
    return (seg_owner, seg_place)


def layer_norm(value, gain_row, shift_row):
    center = value - jnp.mean(value, axis=-1, keepdims=True)
    spread = jnp.mean(center * center, axis=-1, keepdims=True)
    return center * lax.rsqrt(spread + EPSILON) * gain_row + shift_row


def gelu_exact(value):
    return jax.nn.gelu(value, approximate=False)


def blocked(matrix, groups):
    return matrix.reshape(groups, matrix.shape[0] // groups, matrix.shape[1] // HEAD, HEAD)


def scores_of(query_blocks, key_blocks, allowed):
    scores = (
        jnp.einsum("gqhe,gkhe->ghqk", query_blocks, key_blocks, preferred_element_type=jnp.float32)
        * 0.125
    )
    if allowed is not None:
        scores = jnp.where(allowed[None, None], scores, -1000000000.0)
    return scores


def attend_forward(query_blocks, key_blocks, value_blocks, allowed):
    scores = scores_of(query_blocks, key_blocks, allowed)
    top_score = jnp.max(scores, axis=-1, keepdims=True)
    log_total = top_score + jnp.log(jnp.sum(jnp.exp(scores - top_score), axis=-1, keepdims=True))
    probs_low = jnp.exp(scores - log_total).astype(jnp.bfloat16)
    attended = jnp.einsum(
        "ghqk,gkhe->gqhe", probs_low, value_blocks, preferred_element_type=jnp.float32
    )
    return (attended, log_total)


def attend_backward(query_blocks, key_blocks, value_blocks, log_total, grad_blocks, allowed):
    probs = jnp.exp(scores_of(query_blocks, key_blocks, allowed) - log_total)
    d_prob = jnp.einsum(
        "gqhe,gkhe->ghqk", grad_blocks, value_blocks, preferred_element_type=jnp.float32
    )
    d_scores = (probs * (d_prob - jnp.sum(probs * d_prob, axis=-1, keepdims=True))).astype(
        jnp.bfloat16
    )
    d_query = (
        jnp.einsum("ghqk,gkhe->gqhe", d_scores, key_blocks, preferred_element_type=jnp.float32)
        * 0.125
    )
    d_keys = (
        jnp.einsum("ghqk,gqhe->gkhe", d_scores, query_blocks, preferred_element_type=jnp.float32)
        * 0.125
    )
    d_values = jnp.einsum(
        "ghqk,gqhe->gkhe",
        probs.astype(jnp.bfloat16),
        grad_blocks,
        preferred_element_type=jnp.float32,
    )
    return (d_query, d_keys, d_values)


def block_forward(value, params, groups, allowed, widen):
    w_qkv, qv_bias, w_out, w_up, up_bias, w_down, gains, shifts = params
    head_width = w_qkv.shape[2]
    row_count = value.shape[0]
    value_low = value.astype(jnp.bfloat16)
    mixed_qkv = jnp.dot(
        value_low, w_qkv.reshape(w_qkv.shape[0], 3 * head_width), preferred_element_type=jnp.float32
    )
    query_rows = (mixed_qkv[:, :head_width] + qv_bias[0]).astype(jnp.bfloat16)
    key_rows = mixed_qkv[:, head_width : 2 * head_width].astype(jnp.bfloat16)
    value_rows = (mixed_qkv[:, 2 * head_width :] + qv_bias[1]).astype(jnp.bfloat16)
    if widen is not None:
        key_rows, value_rows = widen(key_rows, value_rows)
    query_blocks = blocked(query_rows, groups)
    key_blocks = blocked(key_rows, groups)
    value_blocks = blocked(value_rows, groups)
    attended, log_total = attend_forward(query_blocks, key_blocks, value_blocks, allowed)
    attended_low = attended.reshape(row_count, head_width).astype(jnp.bfloat16)
    branch = lax.psum(jnp.dot(attended_low, w_out, preferred_element_type=jnp.float32), "mp")
    resid = value + branch + shifts[0]
    hidden = layer_norm(resid, gains[0], shifts[1])
    hidden_low = hidden.astype(jnp.bfloat16)
    pre_act = jnp.dot(hidden_low, w_up, preferred_element_type=jnp.float32) + up_bias
    act_low = gelu_exact(pre_act).astype(jnp.bfloat16)
    mlp_out = lax.psum(jnp.dot(act_low, w_down, preferred_element_type=jnp.float32), "mp")
    second = hidden + mlp_out + shifts[2]
    result = layer_norm(second, gains[1], shifts[3])
    saved_state = (
        value_low,
        query_blocks,
        key_blocks,
        value_blocks,
        log_total,
        attended_low,
        resid,
        hidden_low,
        pre_act,
        act_low,
        second,
    )
    return (result, saved_state)


def block_backward(grad_out, saved_state, params, groups, allowed, narrow):
    w_qkv, qv_bias, w_out, w_up, up_bias, w_down, gains, shifts = params
    (
        value_low,
        query_blocks,
        key_blocks,
        value_blocks,
        log_total,
        attended_low,
        resid,
        hidden_low,
        pre_act,
        act_low,
        second,
    ) = saved_state
    row_count = value_low.shape[0]
    head_width = w_qkv.shape[2]
    second_pull = jax.vjp(layer_norm, second, gains[1], shifts[3])[1]
    d_second, d_gain_mlp, d_shift_mlp = second_pull(grad_out)
    second_low = d_second.astype(jnp.bfloat16)
    grad_down = jnp.dot(act_low.T, second_low, preferred_element_type=jnp.float32)
    d_act = jnp.dot(second_low, w_down.T, preferred_element_type=jnp.float32)
    d_pre = jax.vjp(gelu_exact, pre_act)[1](d_act)[0].astype(jnp.bfloat16)
    grad_up = jnp.dot(hidden_low.T, d_pre, preferred_element_type=jnp.float32)
    grad_up_bias = jnp.sum(d_pre, axis=0, dtype=jnp.float32)
    first_pull = jax.vjp(layer_norm, resid, gains[0], shifts[1])[1]
    d_hidden = lax.psum(jnp.dot(d_pre, w_up.T, preferred_element_type=jnp.float32), "mp") + d_second
    d_resid, d_gain_attn, d_shift_attn = first_pull(d_hidden)
    resid_shift = jnp.sum(d_resid, axis=0)
    resid_low = d_resid.astype(jnp.bfloat16)
    grad_out_proj = jnp.dot(attended_low.T, resid_low, preferred_element_type=jnp.float32)
    d_attended = jnp.dot(resid_low, w_out.T, preferred_element_type=jnp.float32).astype(
        jnp.bfloat16
    )
    d_query, d_keys, d_values = attend_backward(
        query_blocks, key_blocks, value_blocks, log_total, blocked(d_attended, groups), allowed
    )
    d_query = d_query.reshape(row_count, head_width)
    d_keys = d_keys.reshape(-1, head_width)
    d_values = d_values.reshape(-1, head_width)
    if narrow is not None:
        d_keys, d_values = narrow(d_keys, d_values)
    d_mixed = jnp.concatenate([d_query, d_keys, d_values], axis=1).astype(jnp.bfloat16)
    grad_qkv = jnp.dot(value_low.T, d_mixed, preferred_element_type=jnp.float32).reshape(
        value_low.shape[1], 3, head_width
    )
    grad_qv_bias = jnp.stack(
        [
            jnp.sum(d_mixed[:, :head_width], axis=0, dtype=jnp.float32),
            jnp.sum(d_mixed[:, 2 * head_width :], axis=0, dtype=jnp.float32),
        ]
    )
    flat_qkv = w_qkv.reshape(w_qkv.shape[0], 3 * head_width)
    d_value = (
        lax.psum(jnp.dot(d_mixed, flat_qkv.T, preferred_element_type=jnp.float32), "mp") + d_resid
    )
    grad_gains = jnp.stack([d_gain_attn, d_gain_mlp])
    grad_shifts = jnp.stack([resid_shift, d_shift_attn, jnp.sum(d_second, axis=0), d_shift_mlp])
    return (
        d_value,
        (
            grad_qkv,
            grad_qv_bias,
            grad_out_proj,
            grad_up,
            grad_up_bias,
            grad_down,
            grad_gains,
            grad_shifts,
        ),
    )


def shards(
    tokens,
    seg_counts,
    seg_order,
    seg_qkv,
    seg_qv_bias,
    seg_out,
    seg_up,
    seg_up_bias,
    seg_down,
    seg_gains,
    seg_shifts,
    cls_qkv,
    cls_qv_bias,
    cls_out,
    cls_up,
    cls_up_bias,
    cls_down,
    cls_gains,
    cls_shifts,
    pos_table,
    cotangent,
):
    seg_owner, seg_place = layout(seg_counts, seg_order)
    seg_params = (
        seg_qkv,
        seg_qv_bias,
        seg_out,
        seg_up,
        seg_up_bias,
        seg_down,
        seg_gains,
        seg_shifts,
    )
    cls_params = (
        cls_qkv,
        cls_qv_bias,
        cls_out,
        cls_up,
        cls_up_bias,
        cls_down,
        cls_gains,
        cls_shifts,
    )
    row_count = tokens.shape[0]
    seg_count = row_count // SEG
    first_out, first_state = block_forward(
        tokens.astype(jnp.float32), seg_params, seg_count, None, None
    )
    cls_own = first_out[::SEG]
    cls_cot = cotangent[::SEG].astype(jnp.float32)
    own_start = lax.axis_index("dp") * seg_count
    place_index = jnp.arange(pos_table.shape[0], dtype=jnp.int32)
    own_owner = lax.dynamic_slice_in_dim(seg_owner, own_start, seg_count)
    own_place = lax.dynamic_slice_in_dim(seg_place, own_start, seg_count)
    allowed = own_owner[:, None] == seg_owner[None, :]
    place_hot = (own_place[:, None] == place_index[None, :]).astype(jnp.bfloat16)
    cls_input = cls_own + jnp.dot(place_hot, pos_table, preferred_element_type=jnp.float32)

    def widen(key_rows, value_rows):
        return (
            lax.all_gather(key_rows, "dp", axis=0, tiled=True),
            lax.all_gather(value_rows, "dp", axis=0, tiled=True),
        )

    def narrow(key_grads, value_grads):
        return (
            lax.psum_scatter(key_grads, "dp", scatter_dimension=0, tiled=True),
            lax.psum_scatter(value_grads, "dp", scatter_dimension=0, tiled=True),
        )

    cls_result, cls_state = block_forward(cls_input, cls_params, 1, allowed, widen)
    cls_grad, cls_grads = block_backward(cls_cot, cls_state, cls_params, 1, allowed, narrow)
    pos_grad = jnp.dot(place_hot.astype(jnp.float32).T, cls_grad, precision=lax.Precision.HIGHEST)
    layer_out = first_out.at[::SEG].set(cls_result).astype(jnp.bfloat16)
    first_cot = cotangent.astype(jnp.float32).at[::SEG].set(cls_grad)
    tokens_grad, seg_grads = block_backward(
        first_cot, first_state, seg_params, seg_count, None, None
    )
    summed = lax.psum(
        (
            seg_grads[0],
            seg_grads[1],
            seg_grads[2],
            seg_grads[3],
            seg_grads[4],
            seg_grads[5],
            seg_grads[6],
            seg_grads[7],
            cls_grads[0],
            cls_grads[1],
            cls_grads[2],
            cls_grads[3],
            cls_grads[4],
            cls_grads[5],
            cls_grads[6],
            cls_grads[7],
            pos_grad,
        ),
        "dp",
    )
    seg_total = summed[:8]
    cls_total = summed[8:16]
    pos_total = summed[16]
    return (
        layer_out,
        tokens_grad,
        seg_total[0],
        seg_total[1],
        seg_total[2],
        seg_total[3],
        seg_total[4],
        seg_total[5],
        seg_total[6],
        seg_total[7],
        cls_total[0],
        cls_total[1],
        cls_total[2],
        cls_total[3],
        cls_total[4],
        cls_total[5],
        cls_total[6],
        cls_total[7],
        pos_total,
    )


def solution(mesh):
    in_specs = (
        P("dp", None),
        P(),
        P(),
        P(None, None, "mp"),
        P(None, "mp"),
        P("mp", None),
        P(None, "mp"),
        P("mp"),
        P("mp", None),
        P(),
        P(),
        P(None, None, "mp"),
        P(None, "mp"),
        P("mp", None),
        P(None, "mp"),
        P("mp"),
        P("mp", None),
        P(),
        P(),
        P(),
        P("dp", None),
    )
    out_specs = (
        P("dp", None),
        P("dp", None),
        P(None, None, "mp"),
        P(None, "mp"),
        P("mp", None),
        P(None, "mp"),
        P("mp"),
        P("mp", None),
        P(),
        P(),
        P(None, None, "mp"),
        P(None, "mp"),
        P("mp", None),
        P(None, "mp"),
        P("mp"),
        P("mp", None),
        P(),
        P(),
        P(),
    )
    return jax.shard_map(shards, mesh=mesh, in_specs=in_specs, out_specs=out_specs, check_vma=False)
```

profile of v0, /device:TPU:0, one launch (start us, length us, event | category | flops | bytes accessed | tf_op | source)
XLA Modules:
  0.0 1121.3 jit_solution(4700022063488982051)
XLA Ops:
  8.0 2.7 fusion.114
  13.5 2.3 fusion.26
  21.1 2.5 fusion.84
  29.0 3.2 compare_reduce_fusion
  32.3 54.8 %all-reduce.8.cloned.1.call-done = f32[1024,768]{1,0:T(8,128)} async-done(((f32[1024,768]{1,0:T(8,128)}), f32[1024,768]{1,0:T(8,128)}) %all-reduce.8.cloned.1.call-update) | async-done | bytes 3145744 | tf_op jit(solution)/shard_map/psum | solution.py:119
  87.1 2.8 fusion.106
  90.7 9.6 multiply_convert_fusion
  101.5 3.1 fusion.115
  104.7 3.1 compare_select_fusion.2
  107.8 3.3 convert_element_type.149
  114.3 3.9 compare_select_fusion.3
  119.8 3.9 fusion.161
  129.6 43.7 %all-reduce.10.cloned.1.call-done = f32[1024,768]{1,0:T(8,128)} async-done(((f32[1024,768]{1,0:T(8,128)}), f32[1024,768]{1,0:T(8,128)}) %all-reduce.10.cloned.1.call-update) | async-done | bytes 3145744 | tf_op jit(solution)/shard_map/psum | solution.py:125
  173.3 3.9 fusion.104
  179.0 2.2 multiply_add_fusion
  181.2 2.5 slice.101
  188.9 31.7 %all_gather.6 = bf16[64,192]{1,0:T(8,128)(2,1)} all-gather(bf16[8,192]{1,0:T(8,128)(2,1)S(1)} %get-tuple-element.99), channel_id=1, replica_groups=mesh['dp'=8,'mp'=4] {'dp'}, dimensions={0}, use_global_device_ids=true | all-gather | bytes 27648 | tf_op jit(solution)/shard_map/all_gather | solution.py:279
  222.0 31.8 %all_gather.7 = bf16[64,192]{1,0:T(8,128)(2,1)} all-gather(bf16[8,192]{1,0:T(8,128)(2,1)} %slice.155), channel_id=1, replica_groups=mesh['dp'=8,'mp'=4] {'dp'}, dimensions={0}, use_global_device_ids=true | all-gather | bytes 27648 | tf_op jit(solution)/shard_map/all_gather | solution.py:278
  263.0 11.7 %psum.177 = f32[8,768]{1,0:T(8,128)} all-reduce(f32[8,768]{1,0:T(8,128)} %fusion.116), channel_id=1, replica_groups=mesh['dp'=8,'mp'=4] {'mp'}, use_global_device_ids=true, to_apply=%region_18.19 | all-reduce | flops 6144 | bytes 49152 | tf_op jit(solution)/shard_map/psum | solution.py:119
  276.4 2.2 multiply_convert_fusion.2
  279.2 2.2 fusion.117
  281.4 11.6 %psum.178 = f32[8,768]{1,0:T(8,128)} all-reduce(f32[8,768]{1,0:T(8,128)} %fusion.117), channel_id=1, replica_groups=mesh['dp'=8,'mp'=4] {'mp'}, use_global_device_ids=true, to_apply=%region_21.22 | all-reduce | flops 6144 | bytes 49152 | tf_op jit(solution)/shard_map/psum | solution.py:125
  297.0 2.3 convert_reduce_fusion.4
  300.0 2.3 fusion.118
  302.3 11.4 %psum.179 = f32[8,768]{1,0:T(8,128)} all-reduce(f32[8,768]{1,0:T(8,128)} %fusion.118), channel_id=1, replica_groups=mesh['dp'=8,'mp'=4] {'mp'}, use_global_device_ids=true, to_apply=%region_27.28 | all-reduce | flops 6144 | bytes 49152 | tf_op jit(solution)/shard_map/psum | solution.py:170
  322.1 2.1 multiply_reduce_fusion.11
  333.5 54.3 %reduce-scatter.5.cloned.1.call-done = f32[8,192]{1,0:T(8,128)} async-done(((f32[64,192]{1,0:T(8,128)}), f32[8,192]{1,0:T(8,128)}) %reduce-scatter.5.cloned.1.call-update) | async-done | bytes 6160 | tf_op jit(solution)/shard_map/reduce_scatter | solution.py:285
  389.7 62.3 %reduce-scatter.3.cloned.1.call-done = f32[8,192]{1,0:T(8,128)} async-done(((f32[64,192]{1,0:T(8,128)}), f32[8,192]{1,0:T(8,128)}) %reduce-scatter.3.cloned.1.call-update) | async-done | bytes 6160 | tf_op jit(solution)/shard_map/reduce_scatter | solution.py:284
  453.2 2.1 fusion.78
  455.3 11.4 %psum.180 = f32[8,768]{1,0:T(8,128)} all-reduce(f32[8,768]{1,0:T(8,128)} %fusion.78), channel_id=1, replica_groups=mesh['dp'=8,'mp'=4] {'mp'}, use_global_device_ids=true, to_apply=%region_33.34 | all-reduce | flops 6144 | bytes 49152 | tf_op jit(solution)/shard_map/psum | solution.py:198
  466.7 4.4 scatter_custom_fusion.1
  471.2 4.4 multiply_reduce_fusion
  478.1 2.1 copy-done.121
  480.2 3.2 convert_reduce_fusion
  484.6 3.1 fusion.119
  496.3 59.4 %all-reduce.12.cloned.1.call-done = f32[1024,768]{1,0:T(8,128)} async-done(((f32[1024,768]{1,0:T(8,128)}), f32[1024,768]{1,0:T(8,128)}) %all-reduce.12.cloned.1.call-update) | async-done | bytes 3145744 | tf_op jit(solution)/shard_map/psum | solution.py:170
  555.8 5.4 multiply_reduce_fusion.1
  567.9 3.1 fusion.120
  571.6 5.5 fusion.95
  577.2 3.3 fusion.111
  582.4 2.3 fusion.121
  585.5 4.4 scatter_custom_fusion
  590.0 3.3 convert_element_type.148
  594.0 45.7 %all-reduce.14.cloned.1.call-done = f32[1024,768]{1,0:T(8,128)} async-done(((f32[1024,768]{1,0:T(8,128)}), f32[1024,768]{1,0:T(8,128)}) %all-reduce.14.cloned.1.call-update) | async-done | bytes 3145744 | tf_op jit(solution)/shard_map/psum | solution.py:198
  639.7 4.9 add_reduce_fusion
  644.7 39.9 %all-reduce = (f32[2,192]{1,0:T(2,128)}, f32[768]{0:T(1024)}, f32[2,768]{1,0:T(2,128)}, f32[4,768]{1,0:T(4,128)}, f32[2,192]{1,0:T(2,128)}, /*index=5*/f32[768]{0:T(1024)}, f32[2,768]{1,0:T(2,128)}, f32[4,768]{1,0:T(4,128)}) all-reduce(f32[2,192]{1,0:T(2,128)S(1)} %get-tuple-element.123, ...), channel_id=1, replica_groups=mesh['dp'=8,'mp'=4] {'dp'}, use_global_device_ids=true, to_apply=%region_45.46 | all-reduce | flops 11520 | bytes 92160 | tf_op jit(solution)/shard_map/psum | solution.py:296
  684.5 416.4 %all-reduce.16.cloned.1.call-done = (f32[768,3,192]{0,2,1:T(8,128)}, f32[192,768]{1,0:T(8,128)}, f32[768,768]{1,0:T(8,128)}, f32[768,768]{1,0:T(8,128)}, f32[768...) async-done(((f32[768,3,192]{0,2,1:T(8,128)}, f32[192,768]{1,0:T(8,128)}, f32[768,768]{1,0:T(8,128)}, ...) | async-done | bytes 14352400 | tf_op jit(solution)/shard_map/psum | solution.py:296
  1100.9 2.9 copy.205
  (386 shorter events, 104.5 us)
Async XLA Ops:
  7.2 83.3 %copy-start = (bf16[768,768]{1,0:T(8,128)(2,1)S(1)}, bf16[768,768]{1,0:T(8,128)(2,1)}, u32[]{:S(2)}) copy-start(bf16[768,768]{1,0:T(8,128)(2,1)} %param.27) | copy-start | bytes 3538948
  7.2 79.9 %all-reduce.8.cloned.1.call-start = ((), (), s32[]{:S(2)}) async-start(), calls=%async_computation.2 | async-start | bytes 6291456 | tf_op jit(solution)/shard_map/psum | solution.py:119
  15.8 157.6 %all-reduce.10.cloned.1.call-start = ((), (), s32[]{:S(2)}) async-start(), calls=%async_computation.3 | async-start | bytes 6291456 | tf_op jit(solution)/shard_map/psum | solution.py:125
  89.9 10.4 copy-start.4
  90.0 10.4 copy-start.46
  90.5 9.9 copy-start.72
  90.5 9.9 copy-start.56
  90.7 10.8 copy-start.112
  104.6 283.2 %reduce-scatter.5.cloned.1.call-start = ((), (), s32[]{:S(2)}) async-start(), calls=%async_computation.5 | async-start | bytes 73728 | tf_op jit(solution)/shard_map/reduce_scatter | solution.py:285
  325.9 126.1 %reduce-scatter.3.cloned.1.call-start = ((), (), s32[]{:S(2)}) async-start(), calls=%async_computation.4 | async-start | bytes 73728 | tf_op jit(solution)/shard_map/reduce_scatter | solution.py:284
  333.4 222.3 %all-reduce.12.cloned.1.call-start = ((), (), s32[]{:S(2)}) async-start(), calls=%async_computation.6 | async-start | bytes 6291456 | tf_op jit(solution)/shard_map/psum | solution.py:170
  471.1 4.4 copy-start.75
  471.1 4.4 copy-start.3
  471.1 4.7 copy-start.9
  471.1 4.7 copy-start.50
  471.1 4.7 copy-start.55
  471.1 4.7 copy-start.60
  475.9 4.3 copy-start.121
  477.4 6.0 copy-start.10
  477.4 6.0 copy-start.89
  487.7 3.8 copy-start.22
  487.7 3.8 copy-start.39
  487.7 3.8 copy-start.45
  487.7 3.8 copy-start.63
  487.7 3.8 copy-start.77
  487.8 5.8 copy-start.36
  487.8 5.8 copy-start.110
  487.8 6.8 copy-start.33
  487.8 6.8 copy-start.64
  487.8 6.8 copy-start.70
  487.8 6.8 copy-start.71
  487.8 151.8 %all-reduce.14.cloned.1.call-start = ((), (), s32[]{:S(2)}) async-start(), calls=%async_computation.7 | async-start | bytes 6291456 | tf_op jit(solution)/shard_map/psum | solution.py:198
  489.6 66.2 %copy-start.47 = (f32[1024]{0:T(1024)S(1)}, f32[1024]{0:T(1024)}, u32[]{:S(2)}) copy-start(f32[1024]{0:T(1024)} %copy-done.46) | copy-start | bytes 12292
  489.6 66.2 %copy-start.52 = (f32[768]{0:T(1024)S(1)}, f32[768]{0:T(1024)}, u32[]{:S(2)}) copy-start(f32[768]{0:T(1024)} %get-tuple-element.48) | copy-start | bytes 9220
  489.6 66.2 %copy-start.57 = (f32[1024]{0:T(1024)S(1)}, f32[1024]{0:T(1024)}, u32[]{:S(2)}) copy-start(f32[1024]{0:T(1024)} %copy-done.56) | copy-start | bytes 12292
  489.6 66.2 %copy-start.90 = (f32[1024]{0:T(1024)S(1)}, f32[1024]{0:T(1024)}, u32[]{:S(2)}) copy-start(f32[1024]{0:T(1024)} %copy-done.89) | copy-start | bytes 12292
  496.3 64.9 %copy-start.73 = (f32[1024]{0:T(1024)S(1)}, f32[1024]{0:T(1024)}, u32[]{:S(2)}) copy-start(f32[1024]{0:T(1024)} %copy-done.72) | copy-start | bytes 12292
  555.7 5.5 copy-start.5
  571.0 6.1 copy-start.48
  571.0 6.1 copy-start.53
  571.0 6.1 copy-start.58
  571.0 6.1 copy-start.80
  571.0 529.9 %all-reduce.16.cloned.1.call-start = ((), (), s32[]{:S(2)}) async-start(), calls=%async_computation.8 | async-start | bytes 28704768 | tf_op jit(solution)/shard_map/psum | solution.py:296
  571.6 5.5 copy-start.6
  571.6 5.5 copy-start.119
  590.0 3.9 copy-start.109
  594.0 50.7 %copy-start.82 = (f32[768]{0:T(1024)S(1)}, f32[768]{0:T(1024)}, u32[]{:S(2)}) copy-start(f32[768]{0:T(1024)} %get-tuple-element.117) | copy-start | bytes 9220
  594.0 50.7 %copy-start.108 = (f32[768]{0:T(1024)S(1)}, f32[768]{0:T(1024)}, u32[]{:S(2)}) copy-start(f32[768]{0:T(1024)} %get-tuple-element.115) | copy-start | bytes 9220
  (81 other events, 153.7 us)
Sparse Core Ops, SparseCore 0:
  15.9 71.1 all-reduce.7
  104.8 68.5 all-reduce.9
  326.0 61.7 reduce-scatter.4
  391.6 60.2 reduce-scatter.2
  487.9 67.7 all-reduce.11
  571.1 68.5 all-reduce.13
  647.6 453.3 all-reduce.15
where the time goes:
time: 1120 us
  waiting for transfers between devices  737 us (66%)
  blocking collectives  149 us (13%)
  other arithmetic  81.9 us (7%)
  matrix products  76.6 us (7%)
  local copies, waits for them, and re-layouts  59.7 us (5%)
  between operations  16.2 us (1%)
    psum x1, waiting for transfers between devices, shards(): lax.psum((seg_grads[0], seg_grads[1], seg_grads[2], seg_grads[3], seg_gra...  416 us
    reduce_scatter x1, waiting for transfers between devices, narrow(): lax.psum_scatter(key_grads, 'dp', scatter_dimension=0, tiled=True)  62.3 us
    psum x1, waiting for transfers between devices, block_backward(): lax.psum(jnp.dot(d_pre, w_up.T, preferred_element_type=jnp.float32), 'mp')  59.4 us
    psum x1, waiting for transfers between devices, block_forward(): lax.psum(jnp.dot(attended_low, w_out, preferred_element_type=jnp.float32)...  54.8 us
    reduce_scatter x1, waiting for transfers between devices, narrow(): lax.psum_scatter(value_grads, 'dp', scatter_dimension=0, tiled=True)  54.3 us
    psum x1, waiting for transfers between devices, block_backward(): lax.psum(jnp.dot(d_mixed, flat_qkv.T, preferred_element_type=jnp.float32)...  45.7 us
    psum x1, waiting for transfers between devices, block_forward(): lax.psum(jnp.dot(act_low, w_down, preferred_element_type=jnp.float32), 'mp')  43.7 us
    psum x1, blocking collectives, shards(): lax.psum((seg_grads[0], seg_grads[1], seg_grads[2], seg_grads[3], seg_gra...  39.9 us
  transfers between devices with their start and end apart: 7, of which 7 were waited for; matrix products, arithmetic and copies ran while one was open for 7% of the time, Pallas kernels for 0%

commit v1 on v0

v1 whole, which is shorter than its diff:
```python
import jax
import jax.numpy as jnp
from jax import lax
from jax.sharding import PartitionSpec as P

HEAD = 64
SEG = 128
EPSILON = 1e-05
BF = jnp.bfloat16
F32 = jnp.float32


def layout(seg_counts, seg_order):
    slot_total = seg_order.shape[0]
    doc_index = jnp.arange(seg_counts.shape[0], dtype=jnp.int32)
    upto = doc_index[:, None] >= doc_index[None, :]
    doc_ends = jnp.sum(jnp.where(upto, seg_counts[None, :], 0), axis=1)
    doc_starts = doc_ends - seg_counts
    longest = jnp.argmax(seg_counts)
    chosen = doc_index == longest
    lead_seg = jnp.sum(jnp.where(chosen, doc_starts, 0))
    trail_seg = jnp.sum(jnp.where(chosen, doc_ends, 0)) - 1
    slot_index = jnp.arange(slot_total, dtype=jnp.int32)
    slot_seg = jnp.where(
        slot_index == 0, lead_seg, jnp.where(seg_order == lead_seg, seg_order[0], seg_order)
    )
    slot_seg = jnp.where(
        slot_index == slot_total - 1,
        trail_seg,
        jnp.where(slot_seg == trail_seg, slot_seg[slot_total - 1], slot_seg),
    )
    seg_owner = jnp.sum((slot_seg[:, None] >= doc_ends[None, :]).astype(jnp.int32), axis=1)
    seg_start = jnp.sum(
        jnp.where(seg_owner[:, None] == doc_index[None, :], doc_starts[None, :], 0), axis=1
    )
    return (seg_owner, slot_seg - seg_start)


def dot(a, b):
    return jnp.dot(a, b, preferred_element_type=F32)


def dot_t(a, b):
    return lax.dot_general(a, b, (((1,), (1,)), ((), ())), preferred_element_type=F32)


def t_dot(a, b):
    return lax.dot_general(a, b, (((0,), (0,)), ((), ())), preferred_element_type=F32)


def norm_parts(value):
    center = value - jnp.mean(value, axis=-1, keepdims=True)
    rstd = lax.rsqrt(jnp.mean(center * center, axis=-1, keepdims=True) + EPSILON)
    return center * rstd, rstd


def norm_back(grad, normed, rstd, gain):
    gy = grad * gain
    return rstd * (
        gy - jnp.mean(gy, axis=-1, keepdims=True) - normed * jnp.mean(gy * normed, axis=-1, keepdims=True)
    )


def gelu_both(pre):
    phi_cdf = 0.5 * (1.0 + lax.erf(pre * 0.7071067811865476))
    phi_pdf = 0.3989422804014327 * jnp.exp(-0.5 * pre * pre)
    return pre * phi_cdf, phi_cdf + pre * phi_pdf


def heads_of(matrix, groups):
    return matrix.reshape(groups, matrix.shape[0] // groups, matrix.shape[1] // HEAD, HEAD)


def scores_of(query, keys, allowed):
    scores = jnp.einsum("gqhe,gkhe->ghqk", query, keys, preferred_element_type=F32) * 0.125
    if allowed is not None:
        scores = jnp.where(allowed[None, None], scores, -1000000000.0)
    return scores


def attend(query, keys, values, allowed):
    scores = scores_of(query, keys, allowed)
    top = jnp.max(scores, axis=-1, keepdims=True)
    powers = jnp.exp(scores - top)
    probs = powers / jnp.sum(powers, axis=-1, keepdims=True)
    attended = jnp.einsum("ghqk,gkhe->gqhe", probs.astype(BF), values, preferred_element_type=F32)
    return attended.astype(BF)


def attend_back(query, keys, values, grad, allowed):
    scores = scores_of(query, keys, allowed)
    top = jnp.max(scores, axis=-1, keepdims=True)
    powers = jnp.exp(scores - top)
    probs = powers / jnp.sum(powers, axis=-1, keepdims=True)
    d_prob = jnp.einsum("gqhe,gkhe->ghqk", grad, values, preferred_element_type=F32)
    d_scores = (probs * (d_prob - jnp.sum(probs * d_prob, axis=-1, keepdims=True))).astype(BF)
    d_query = jnp.einsum("ghqk,gkhe->gqhe", d_scores, keys, preferred_element_type=F32) * 0.125
    d_keys = jnp.einsum("ghqk,gqhe->gkhe", d_scores, query, preferred_element_type=F32) * 0.125
    d_values = jnp.einsum("ghqk,gqhe->gkhe", probs.astype(BF), grad, preferred_element_type=F32)
    return d_query, d_keys, d_values


def make_shards(n_dp):
    core_pairs = [(i, i ^ 1) for i in range(4)]
    x_pairs = [(i, i ^ 2) for i in range(4)]

    def core_swap(value):
        return lax.ppermute(value, "mp", core_pairs)

    def x_swap(value):
        return lax.ppermute(value, "mp", x_pairs)

    def x_sum_low(partial):
        mine = partial.astype(BF)
        return mine.astype(F32) + x_swap(mine).astype(F32)

    def x_sum(partial):
        return partial + x_swap(partial)

    def shards(
        tokens,
        seg_counts,
        seg_order,
        seg_qkv,
        seg_qv_bias,
        seg_out,
        seg_up,
        seg_up_bias,
        seg_down,
        seg_gains,
        seg_shifts,
        cls_qkv,
        cls_qv_bias,
        cls_out,
        cls_up,
        cls_up_bias,
        cls_down,
        cls_gains,
        cls_shifts,
        pos_table,
        cotangent,
    ):
        core = lax.axis_index("mp") % 2
        dp_index = lax.axis_index("dp")
        first_core = core == 0
        row_count = tokens.shape[0] // 2
        own_segs = row_count // SEG
        slots = seg_order.shape[0]
        width = seg_qkv.shape[2]
        model = tokens.shape[1]

        def paired(value, axis):
            other = core_swap(value)
            return jnp.where(
                first_core,
                jnp.concatenate([value, other], axis=axis),
                jnp.concatenate([other, value], axis=axis),
            )

        def gather_slots(value):
            value = paired(value, 0)
            bit = 1
            while bit < n_dp:
                other = lax.ppermute(value, "dp", [(i, i ^ bit) for i in range(n_dp)])
                value = jnp.where(
                    (dp_index & bit) == 0,
                    jnp.concatenate([value, other], axis=0),
                    jnp.concatenate([other, value], axis=0),
                )
                bit *= 2
            return value

        def own_half(value, axis):
            size = value.shape[axis] // 2
            return lax.dynamic_slice_in_dim(value, core * size, size, axis)

        def other_half(value, axis):
            size = value.shape[axis] // 2
            return lax.dynamic_slice_in_dim(value, (1 - core) * size, size, axis)

        def dp_sum(value, bits):
            for bit in bits:
                rows = value.shape[0] // 2
                side = jnp.where((dp_index & bit) == 0, 0, 1)
                keep = lax.dynamic_slice_in_dim(value, side * rows, rows, 0)
                send = lax.dynamic_slice_in_dim(value, (1 - side) * rows, rows, 0)
                got = lax.ppermute(send, "dp", [(i, i ^ bit) for i in range(n_dp)])
                value = (keep.astype(F32) + got.astype(F32)).astype(BF)
            for bit in reversed(bits):
                got = lax.ppermute(value, "dp", [(i, i ^ bit) for i in range(n_dp)])
                value = jnp.where(
                    (dp_index & bit) == 0,
                    jnp.concatenate([value, got], axis=0),
                    jnp.concatenate([got, value], axis=0),
                )
            return value.astype(F32)

        def core_scatter(value, axis):
            return own_half(value, axis) + core_swap(other_half(value, axis).astype(BF)).astype(F32)

        seg_owner, seg_place = layout(seg_counts, seg_order)
        allowed = seg_owner[:, None] == seg_owner[None, :]
        place_hot = (
            seg_place[:, None] == jnp.arange(pos_table.shape[0], dtype=jnp.int32)[None, :]
        ).astype(BF)

        s_qkv = paired(seg_qkv, 2)
        s_out = paired(seg_out, 0)
        s_up = paired(seg_up, 1)
        s_down = paired(seg_down, 0)
        s_qv_bias = paired(seg_qv_bias, 1)
        s_up_bias = paired(seg_up_bias, 0)
        c_qkv = paired(cls_qkv, 2)
        c_out = paired(cls_out, 0)
        c_up = paired(cls_up, 1)
        c_down = paired(cls_down, 0)
        c_qv_bias = paired(cls_qv_bias, 1)
        c_up_bias = paired(cls_up_bias, 0)
        pair = 2 * width
        s_qkv_flat = s_qkv.reshape(model, 3 * pair)
        c_qkv_flat = c_qkv.reshape(model, 3 * pair)

        rows_low = own_half(tokens, 0)
        mixed = dot(rows_low, s_qkv_flat)
        query = heads_of((mixed[:, :pair] + s_qv_bias[0]).astype(BF), own_segs)
        keys = heads_of(mixed[:, pair : 2 * pair].astype(BF), own_segs)
        values = heads_of((mixed[:, 2 * pair :] + s_qv_bias[1]).astype(BF), own_segs)
        attended = attend(query, keys, values, None).reshape(row_count, pair)
        branch = x_sum_low(dot(attended, s_out))
        resid = rows_low.astype(F32) + branch + seg_shifts[0]

        lead_resid = gather_slots(resid[::SEG])
        lead_attended = gather_slots(attended[::SEG])
        lead_n1, lead_rstd1 = norm_parts(lead_resid)
        lead_hidden = lead_n1 * seg_gains[0] + seg_shifts[1]
        lead_hidden_low = lead_hidden.astype(BF)
        lead_act, lead_slope = gelu_both(dot(lead_hidden_low, s_up) + s_up_bias)
        lead_act_low = lead_act.astype(BF)
        lead_second = lead_hidden + x_sum(dot(lead_act_low, s_down)) + seg_shifts[2]
        lead_n2, lead_rstd2 = norm_parts(lead_second)
        lead_first = lead_n2 * seg_gains[1] + seg_shifts[3]

        n1, rstd1 = norm_parts(resid)
        hidden = n1 * seg_gains[0] + seg_shifts[1]
        hidden_low = hidden.astype(BF)
        act, slope = gelu_both(dot(hidden_low, s_up) + s_up_bias)
        act_low = act.astype(BF)
        second = hidden + x_sum_low(dot(act_low, s_down)) + seg_shifts[2]
        n2, rstd2 = norm_parts(second)
        first = n2 * seg_gains[1] + seg_shifts[3]

        c_value = lead_first + dot(place_hot, pos_table)
        c_low = c_value.astype(BF)
        c_mixed = dot(c_low, c_qkv_flat)
        c_query = heads_of((c_mixed[:, :pair] + c_qv_bias[0]).astype(BF), 1)
        c_keys = heads_of(c_mixed[:, pair : 2 * pair].astype(BF), 1)
        c_values = heads_of((c_mixed[:, 2 * pair :] + c_qv_bias[1]).astype(BF), 1)
        c_attended = attend(c_query, c_keys, c_values, allowed).reshape(slots, pair)
        c_resid = c_value + x_sum(dot(c_attended, c_out)) + cls_shifts[0]
        c_n1, c_rstd1 = norm_parts(c_resid)
        c_hidden = c_n1 * cls_gains[0] + cls_shifts[1]
        c_hidden_low = c_hidden.astype(BF)
        c_act, c_slope = gelu_both(dot(c_hidden_low, c_up) + c_up_bias)
        c_act_low = c_act.astype(BF)
        c_second = c_hidden + x_sum(dot(c_act_low, c_down)) + cls_shifts[2]
        c_n2, c_rstd2 = norm_parts(c_second)
        c_result = c_n2 * cls_gains[1] + cls_shifts[3]

        own_cot = own_half(cotangent, 0).astype(F32)
        c_gy = gather_slots(own_cot[::SEG])
        c_d_second = norm_back(c_gy, c_n2, c_rstd2, cls_gains[1])
        c_d_second_low = c_d_second.astype(BF)
        c_d_pre = (dot_t(c_d_second_low, c_down) * c_slope).astype(BF)
        c_d_hidden = x_sum(dot_t(c_d_pre, c_up)) + c_d_second
        c_d_resid = norm_back(c_d_hidden, c_n1, c_rstd1, cls_gains[0])
        c_d_resid_low = c_d_resid.astype(BF)
        c_d_attended = dot_t(c_d_resid_low, c_out).astype(BF)
        c_dq, c_dk, c_dv = attend_back(c_query, c_keys, c_values, heads_of(c_d_attended, 1), allowed)
        c_d_mixed = jnp.concatenate(
            [part.reshape(slots, pair) for part in (c_dq, c_dk, c_dv)], axis=1
        ).astype(BF)
        c_grad = x_sum(dot_t(c_d_mixed, c_qkv_flat)) + c_d_resid
        own_c_mixed = own_half(c_d_mixed.reshape(slots, 3, pair), 2)
        cls_grads = (
            t_dot(c_low, own_c_mixed.reshape(slots, 3 * width)).reshape(model, 3, width),
            jnp.sum(own_c_mixed.astype(F32), axis=0)[::2],
            t_dot(own_half(c_attended, 1), c_d_resid_low),
            t_dot(c_hidden_low, own_half(c_d_pre, 1)),
            jnp.sum(own_half(c_d_pre, 1).astype(F32), axis=0),
            t_dot(own_half(c_act_low, 1), c_d_second_low),
            jnp.stack([jnp.sum(c_d_hidden * c_n1, axis=0), jnp.sum(c_gy * c_n2, axis=0)]),
            jnp.stack(
                [
                    jnp.sum(c_d_resid, axis=0),
                    jnp.sum(c_d_hidden, axis=0),
                    jnp.sum(c_d_second, axis=0),
                    jnp.sum(c_gy, axis=0),
                ]
            ),
        )
        pos_grad = jnp.dot(place_hot.astype(F32).T, c_grad, precision=lax.Precision.HIGHEST)

        row_index = lax.broadcasted_iota(jnp.int32, (row_count, 1), 0)
        is_lead = (row_index % SEG) == 0
        gy = jnp.where(is_lead, 0.0, own_cot)
        d_second = norm_back(gy, n2, rstd2, seg_gains[1])
        d_second_low = d_second.astype(BF)
        grad_down = t_dot(act_low, d_second_low)
        d_pre = (dot_t(d_second_low, s_down) * slope).astype(BF)
        grad_up = t_dot(hidden_low, d_pre)
        d_hidden = x_sum_low(dot_t(d_pre, s_up)) + d_second
        d_resid = norm_back(d_hidden, n1, rstd1, seg_gains[0])
        d_resid_low = d_resid.astype(BF)
        grad_out = t_dot(attended, d_resid_low)
        d_attended = dot_t(d_resid_low, s_out).astype(BF)
        orders = [1 << k for k in range(n_dp.bit_length() - 1)]
        swapped = [orders[1], orders[0], *orders[2:]]
        grad_down = dp_sum(core_scatter(grad_down, 0).astype(BF), orders)
        grad_up = dp_sum(core_scatter(grad_up, 1).astype(BF), swapped)
        grad_out = dp_sum(core_scatter(grad_out, 0).astype(BF), orders)
        small = jnp.stack(
            [
                jnp.sum(d_hidden * n1, axis=0),
                jnp.sum(gy * n2, axis=0),
                jnp.sum(d_resid, axis=0),
                jnp.sum(d_hidden, axis=0),
                jnp.sum(d_second, axis=0),
                jnp.sum(gy, axis=0),
            ]
        )
        d_pre_sum = jnp.sum(d_pre.astype(F32), axis=0).reshape(-1, model)

        l_gy = c_grad
        l_d_second = norm_back(l_gy, lead_n2, lead_rstd2, seg_gains[1])
        l_d_second_low = l_d_second.astype(BF)
        l_d_pre = (dot_t(l_d_second_low, s_down) * lead_slope).astype(BF)
        l_d_hidden = x_sum(dot_t(l_d_pre, s_up)) + l_d_second
        l_d_resid = norm_back(l_d_hidden, lead_n1, lead_rstd1, seg_gains[0])
        l_d_resid_low = l_d_resid.astype(BF)
        l_d_attended = dot_t(l_d_resid_low, s_out).astype(BF)
        l_small = jnp.stack(
            [
                jnp.sum(l_d_hidden * lead_n1, axis=0),
                jnp.sum(l_gy * lead_n2, axis=0),
                jnp.sum(l_d_resid, axis=0),
                jnp.sum(l_d_hidden, axis=0),
                jnp.sum(l_d_second, axis=0),
                jnp.sum(l_gy, axis=0),
            ]
        )

        own_start = (dp_index * 2 + core) * own_segs

        def with_leads(value, leads):
            mine = lax.dynamic_slice_in_dim(leads, own_start, own_segs, 0)
            spread = jnp.broadcast_to(mine[:, None, :], (own_segs, SEG, mine.shape[1]))
            return jnp.where(is_lead, spread.reshape(row_count, mine.shape[1]), value)

        d_attended = with_leads(d_attended, l_d_attended)
        d_resid = with_leads(d_resid, l_d_resid)
        dq, dk, dv = attend_back(query, keys, values, heads_of(d_attended, own_segs), None)
        d_mixed = jnp.concatenate(
            [part.reshape(row_count, pair) for part in (dq, dk, dv)], axis=1
        ).astype(BF)
        d_rows = x_sum_low(dot_t(d_mixed, s_qkv_flat)) + d_resid
        tokens_grad = paired(d_rows, 0)
        grad_qkv = core_scatter(t_dot(rows_low, d_mixed).reshape(model, 3, pair), 2)
        grad_qkv = dp_sum(grad_qkv.reshape(model, 3 * width).astype(BF), swapped)
        mixed_sum = jnp.sum(d_mixed.astype(F32), axis=0).reshape(3, pair)[::2]
        tail = jnp.concatenate([small, d_pre_sum, mixed_sum.reshape(-1, model)], axis=0)
        tail = tail + core_swap(tail)
        tail = lax.psum(tail, "dp")
        d_pre_total = tail[6 : 6 + d_pre_sum.shape[0]].reshape(-1)
        mixed_total = tail[6 + d_pre_sum.shape[0] :].reshape(2, pair)
        seg_small = tail[:6] + l_small

        seg_grads = (
            grad_qkv.reshape(model, 3, width),
            own_half(mixed_total, 1),
            grad_out + t_dot(own_half(lead_attended, 1), l_d_resid_low),
            grad_up + t_dot(lead_hidden_low, own_half(l_d_pre, 1)),
            own_half(d_pre_total, 0) + jnp.sum(own_half(l_d_pre, 1).astype(F32), axis=0),
            grad_down + t_dot(own_half(lead_act_low, 1), l_d_second_low),
            seg_small[:2],
            seg_small[2:],
        )

        own_result = lax.dynamic_slice_in_dim(c_result, own_start, own_segs, 0)
        spread = jnp.broadcast_to(own_result[:, None, :], (own_segs, SEG, model))
        own_out = jnp.where(is_lead, spread.reshape(row_count, model), first).astype(BF)
        layer_out = paired(own_out, 0)
        return (layer_out, tokens_grad, *seg_grads, *cls_grads, pos_grad)

    return shards


def solution(mesh):
    in_specs = (
        P("dp", None),
        P(),
        P(),
        P(None, None, "mp"),
        P(None, "mp"),
        P("mp", None),
        P(None, "mp"),
        P("mp"),
        P("mp", None),
        P(),
        P(),
        P(None, None, "mp"),
        P(None, "mp"),
        P("mp", None),
        P(None, "mp"),
        P("mp"),
        P("mp", None),
        P(),
        P(),
        P(),
        P("dp", None),
    )
    out_specs = (
        P("dp", None),
        P("dp", None),
        P(None, None, "mp"),
        P(None, "mp"),
        P("mp", None),
        P(None, "mp"),
        P("mp"),
        P("mp", None),
        P(),
        P(),
        P(None, None, "mp"),
        P(None, "mp"),
        P("mp", None),
        P(None, "mp"),
        P("mp"),
        P("mp", None),
        P(),
        P(),
        P(),
    )
    return jax.shard_map(
        make_shards(mesh.shape["dp"]), mesh=mesh, in_specs=in_specs, out_specs=out_specs, check_vma=False
    )
```

time: 1120 us -> 427 us (0.38)
  waiting for transfers between devices: 737 us -> 124 us
  blocking collectives: 149 us -> 37.8 us
  starting transfers between devices: 0.77 us -> 49.7 us
  matrix products: 76.6 us -> 102 us
  other arithmetic: 81.9 us -> 62.1 us
  local copies, waits for them, and re-layouts: 59.7 us -> 39.9 us
  between operations: 16.2 us -> 4.02 us
    psum x5 -> x0, waiting for transfers between devices: 620 us -> none  [the longest x1 416 us: shards(): lax.psum((seg_grads[0], seg_grads[1], seg_grads[2], seg_grads[3], seg_gra...]
    ppermute x0 -> x65, waiting for transfers between devices: none -> 124 us  [the longest x12 48.7 us: dp_sum(): got = lax.ppermute(send, 'dp', [(i, i ^ bit) for i in range(n_dp)])]
    reduce_scatter x2 -> x0, waiting for transfers between devices: 117 us -> none  [the longest x1 62.3 us: narrow(): lax.psum_scatter(key_grads, 'dp', scatter_dimension=0, tiled=True)]
    all_gather x2 -> x0, blocking collectives: 63.5 us -> none  [the longest x1 31.8 us: widen(): lax.all_gather(key_rows, 'dp', axis=0, tiled=True)]
    ppermute x0 -> x65, starting transfers between devices: none -> 49.7 us  [the longest x10 16.1 us: x_swap(): return lax.ppermute(value, 'mp', x_pairs)]
    psum x5 -> x1, blocking collectives: 86 us -> 37.8 us  [shards(): tail = lax.psum(tail, 'dp')]
    dot_general x38 -> x45, matrix products: 76.6 us -> 101 us  [the longest x11 45.2 us: dot_t(): lax.dot_general(a, b, (((1,), (1,)), ((), ())), preferred_element_type=F32)]
    unnamed x260 -> x256, local copies, waits for them, and re-layouts: 29.4 us -> 5.54 us
  transfers between devices with their start and end apart: 7 -> 65, of which waited for: 7 -> 31; matrix products, arithmetic and copies ran while one was open for 7% -> 47% of each run, Pallas kernels for 0% -> 0%
where the time goes in v1:
time: 427 us; the launch traced here: 420 us
  waiting for transfers between devices  124 us (29%)
  matrix products  102 us (24%)
  other arithmetic  62.1 us (15%)
  starting transfers between devices  49.7 us (12%)
  local copies, waits for them, and re-layouts  39.9 us (9%)
  blocking collectives  37.8 us (9%)
    ppermute x12, waiting for transfers between devices, dp_sum(): got = lax.ppermute(send, 'dp', [(i, i ^ bit) for i in range(n_dp)])  48.7 us
    dot_general x11, matrix products, dot_t(): lax.dot_general(a, b, (((1,), (1,)), ((), ())), preferred_element_type=F32)  45.2 us
    ppermute x12, waiting for transfers between devices, dp_sum(): got = lax.ppermute(value, 'dp', [(i, i ^ bit) for i in range(n_dp)])  41.1 us
    psum x1, blocking collectives, shards(): tail = lax.psum(tail, 'dp')  37.8 us
    dot_general x11, matrix products, dot(): return jnp.dot(a, b, preferred_element_type=F32)  24.6 us
    dot_general x11, matrix products, t_dot(): lax.dot_general(a, b, (((0,), (0,)), ((), ())), preferred_element_type=F32)  21.3 us
    ppermute x10, waiting for transfers between devices, x_swap(): return lax.ppermute(value, 'mp', x_pairs)  17.6 us
    ppermute x10, starting transfers between devices, x_swap(): return lax.ppermute(value, 'mp', x_pairs)  16.1 us
  transfers between devices with their start and end apart: 65, of which 31 were waited for; matrix products, arithmetic and copies ran while one was open for 47% of the time, Pallas kernels for 0%

profile of v1, /device:TPU:0, one launch (start us, length us, event | category | flops | bytes accessed | tf_op | source)
XLA Modules:
  0.0 420.0 jit_solution(5983959152226288981)
XLA Ops:
  12.3 2.6 compare_select_fusion.3
  32.7 2.6 convolution_convert_fusion.3
  35.3 2.8 collective-permute-start.3
  51.6 4.7 %collective-permute-done.3 = bf16[512,768]{1,0:T(8,128)(2,1)} collective-permute-done((bf16[512,768]{1,0:T(8,128)(2,1)}, bf16[512,768]{1,0:T(8,128)(2,1)}, u32[]{:S(2)}, u32[]{:S(2)}) %collective-permute-start.3) | collective-permute-done | bytes 786464 | tf_op jit(solution)/shard_map/ppermute | solution.py:111
  70.5 2.5 collective-permute-done.6
  73.0 3.2 collective-permute-start.7
  76.5 3.4 collective-permute-done.7
  82.3 3.4 multiply_convert_fusion.3
  85.7 2.5 fusion.165
  90.3 5.0 %collective-permute-done.11 = f32[64,768]{1,0:T(8,128)S(1)} collective-permute-done((f32[64,768]{1,0:T(8,128)S(1)}, f32[64,768]{1,0:T(8,128)S(1)}, u32[]{:S(2)}, u32[]{:S(2)}) %collective-permute-start.11) | collective-permute-done | bytes 196640 | tf_op jit(solution)/shard_map/ppermute | solution.py:111
  104.4 3.6 multiply_convert_fusion
  109.2 2.5 multiply_convert_fusion.2
  111.7 3.3 fusion.35
  116.5 3.1 convolution_convert_fusion.1
  123.9 3.4 fusion.7
  127.4 16.2 %fusion.36 = f32[64,768]{1,0:T(8,128)} fusion(bf16[64,1536]{1,0:T(8,128)(2,1)S(1)} %fusion.7, bf16[768,768]{1,0:T(8,128)(2,1)} %collective-permute-done.16, bf16[768,768]{1,0:T(8,128)(2,1)S(1)} %copy-done.114, pred[]{:T(512)S(6)} %eq.65), kind=kOutput, calls=%fused_computation.125 | convolution fusion | flops 161611776 | bytes 2752513 | tf_op jit(solution)/shard_map/dot_general | solution.py:44
  143.5 2.5 collective-permute-start.26
  157.5 6.4 %convert_reduce_fusion = (f32[1536]{0:T(1024)S(1)}, bf16[512,1536]{1,0:T(8,128)(2,1)S(1)}) fusion(f32[512,1536]{1,0:T(8,128)S(1)} %get-tuple-element.100, bf16[768,768]{1,0:T(8,128)(2,1)} %collective-permute-done.10, bf16[768,768]{1,0:T(8,128)(2,1)S(1)} %copy-done.116, pred[]{:T(512)S(6)} %eq.65, f32[512,768]{1,0:T(8,128)S(1)} %get-tuple-element.71), kind=kOutput, calls=%fused_computation.10 | convolution fusion | flops 1228405248 | bytes 8656897 | tf_op jit(solution)/shard_map/dot_general | solution.py:44
  163.8 3.8 fusion.162
  167.6 4.0 convolution_convert_fusion
  175.1 2.8 dynamic-slice_convert_fusion.1
  196.4 2.6 fusion.79
  206.9 2.7 collective-permute-done.27
  211.0 2.7 fusion.8
  214.4 2.5 fusion.166
  219.8 3.4 collective-permute-done.28
  226.8 2.3 multiply_reduce_fusion.1
  232.1 2.4 fusion.20
  242.3 3.7 convolution_convert_fusion.2
  247.2 4.5 %maximum_select_fusion.7 = bf16[1024,768]{1,0:T(8,128)(2,1)} fusion(bf16[512,768]{1,0:T(8,128)(2,1)} %collective-permute-done.21, bf16[512,768]{1,0:T(8,128)(2,1)} %fusion.11, pred[]{:T(512)S(6)} %eq.65), kind=kLoop, calls=%fused_computation.36 | loop fusion | flops 7077888 | bytes 3145729 | tf_op jit(solution)/shard_map/jit(_where)/select_n | solution.py:154
  252.8 37.8 %psum.7 = f32[9,768]{1,0:T(8,128)S(1)} all-reduce(f32[9,768]{1,0:T(8,128)S(1)} %add.584), channel_id=1, replica_groups=mesh['dp'=8,'mp'=4] {'dp'}, use_global_device_ids=true, to_apply=%region_44.45 | all-reduce | flops 6912 | bytes 55296 | tf_op jit(solution)/shard_map/psum | solution.py:372
  292.4 4.4 %collective-permute-done.41 = bf16[96,768]{1,0:T(8,128)(2,1)S(1)} collective-permute-done((bf16[96,768]{1,0:T(8,128)(2,1)S(1)}, bf16[96,768]{1,0:T(8,128)(2,1)S(1)}, u32[]{:S(2)}, u32[]{:S(2)}) %collective-permute-start.41) | collective-permute-done | bytes 147488 | tf_op jit(solution)/shard_map/ppermute | solution.py:187
  297.1 4.3 %collective-permute-done.42 = bf16[48,768]{1,0:T(8,128)(2,1)S(1)} collective-permute-done((bf16[48,768]{1,0:T(8,128)(2,1)S(1)}, bf16[48,768]{1,0:T(8,128)(2,1)S(1)}, u32[]{:S(2)}, u32[]{:S(2)}) %collective-permute-start.42) | collective-permute-done | bytes 73760 | tf_op jit(solution)/shard_map/ppermute | solution.py:187
  303.4 3.2 collective-permute-done.43
  310.6 2.7 collective-permute-done.44
  313.4 5.1 %collective-permute-done.45 = bf16[48,768]{1,0:T(8,128)(2,1)S(1)} collective-permute-done((bf16[48,768]{1,0:T(8,128)(2,1)S(1)}, bf16[48,768]{1,0:T(8,128)(2,1)S(1)}, u32[]{:S(2)}, u32[]{:S(2)}) %collective-permute-start.45) | collective-permute-done | bytes 73760 | tf_op jit(solution)/shard_map/ppermute | solution.py:190
  324.5 5.5 %collective-permute-done.46 = bf16[96,768]{1,0:T(8,128)(2,1)S(1)} collective-permute-done((bf16[96,768]{1,0:T(8,128)(2,1)S(1)}, bf16[96,768]{1,0:T(8,128)(2,1)S(1)}, u32[]{:S(2)}, u32[]{:S(2)}) %collective-permute-start.46) | collective-permute-done | bytes 147488 | tf_op jit(solution)/shard_map/ppermute | solution.py:190
  336.1 13.0 %collective-permute-done.60 = bf16[192,768]{1,0:T(8,128)(2,1)S(1)} collective-permute-done((bf16[192,768]{1,0:T(8,128)(2,1)S(1)}, bf16[192,768]{1,0:T(8,128)(2,1)S(1)}, u32[]{:S(2)}, u32[]{:S(2)}) %collective-permute-start.60) | collective-permute-done | bytes 294944 | tf_op jit(solution)/shard_map/ppermute | solution.py:187
  349.9 2.5 collective-permute-start.54
  352.8 12.0 %collective-permute-done.61 = bf16[96,768]{1,0:T(8,128)(2,1)S(1)} collective-permute-done((bf16[96,768]{1,0:T(8,128)(2,1)S(1)}, bf16[96,768]{1,0:T(8,128)(2,1)S(1)}, u32[]{:S(2)}, u32[]{:S(2)}) %collective-permute-start.61) | collective-permute-done | bytes 147488 | tf_op jit(solution)/shard_map/ppermute | solution.py:187
  365.2 3.0 collective-permute-start.35
  368.2 6.1 %collective-permute-done.54 = bf16[96,768]{1,0:T(8,128)(2,1)S(1)} collective-permute-done((bf16[96,768]{1,0:T(8,128)(2,1)S(1)}, bf16[96,768]{1,0:T(8,128)(2,1)S(1)}, u32[]{:S(2)}, u32[]{:S(2)}) %collective-permute-start.54) | collective-permute-done | bytes 147488 | tf_op jit(solution)/shard_map/ppermute | solution.py:187
  374.4 5.6 %collective-permute-done.35 = bf16[96,576]{0,1:T(8,128)(2,1)S(1)} collective-permute-done((bf16[96,576]{0,1:T(8,128)(2,1)S(1)}, bf16[96,576]{0,1:T(8,128)(2,1)S(1)}, u32[]{:S(2)}, u32[]{:S(2)}) %collective-permute-start.35) | collective-permute-done | bytes 110624 | tf_op jit(solution)/shard_map/ppermute | solution.py:187
  380.3 5.9 %collective-permute-done.36 = bf16[96,576]{0,1:T(8,128)(2,1)S(1)} collective-permute-done((bf16[96,576]{0,1:T(8,128)(2,1)S(1)}, bf16[96,576]{0,1:T(8,128)(2,1)S(1)}, u32[]{:S(2)}, u32[]{:S(2)}) %collective-permute-start.36) | collective-permute-done | bytes 110624 | tf_op jit(solution)/shard_map/ppermute | solution.py:190
  389.1 7.5 %collective-permute-done.37 = bf16[192,576]{0,1:T(8,128)(2,1)S(1)} collective-permute-done((bf16[192,576]{0,1:T(8,128)(2,1)S(1)}, bf16[192,576]{0,1:T(8,128)(2,1)S(1)}, u32[]{:S(2)}, u32[]{:S(2)}) %collective-permute-start.37) | collective-permute-done | bytes 221216 | tf_op jit(solution)/shard_map/ppermute | solution.py:190
  397.3 5.6 %collective-permute-done.56 = bf16[192,768]{1,0:T(8,128)(2,1)S(1)} collective-permute-done((bf16[192,768]{1,0:T(8,128)(2,1)S(1)}, bf16[192,768]{1,0:T(8,128)(2,1)S(1)}, u32[]{:S(2)}, u32[]{:S(2)}) %collective-permute-start.56) | collective-permute-done | bytes 294944 | tf_op jit(solution)/shard_map/ppermute | solution.py:190
  405.5 4.5 %collective-permute-done.38 = bf16[384,576]{0,1:T(8,128)(2,1)S(1)} collective-permute-done((bf16[384,576]{0,1:T(8,128)(2,1)S(1)}, bf16[384,576]{0,1:T(8,128)(2,1)S(1)}, u32[]{:S(2)}, u32[]{:S(2)}) %collective-permute-start.38) | collective-permute-done | bytes 442400 | tf_op jit(solution)/shard_map/ppermute | solution.py:190
  414.6 2.9 collective-permute-done.57
  (595 shorter events, 173.2 us)
Async XLA Ops:
  0.7 22.7 %collective-permute-start = (bf16[768,3,192]{0,2,1:T(8,128)(2,1)}, bf16[768,3,192]{0,2,1:T(8,128)(2,1)}, u32[]{:S(2)}, u32[]{:S(2)}) collective-permute-start(bf16[768,3,192]{0,2,1:T(8,128)(2,1)} %param.24), channel_id=1, source_target_pairs={{0,1},{1,0},{2,3},{3,2},{4,5},{5,4},{6,7},{7,6},{8,9},{9,8},{10,11... | collective-permute-start | bytes 2654216 | tf_op jit(solution)/shard_map/ppermute | solution.py:108
  1.2 20.0 %collective-permute-start.1 = (f32[2,192]{1,0:T(2,128)}, f32[2,192]{1,0:T(2,128)S(1)}, u32[]{:S(2)}, u32[]{:S(2)}) collective-permute-start(f32[2,192]{1,0:T(2,128)} %param.25), channel_id=1, source_target_pairs={{0,1},{1,0},{2,3},{3,2},{4,5},{5,4},{6,7},{7,6},{8,9},{9,8},{10,11... | collective-permute-start | bytes 4616 | tf_op jit(solution)/shard_map/ppermute | solution.py:108
  1.3 31.1 %collective-permute-start.2 = (bf16[192,768]{1,0:T(8,128)(2,1)}, bf16[192,768]{1,0:T(8,128)(2,1)}, u32[]{:S(2)}, u32[]{:S(2)}) collective-permute-start(bf16[192,768]{1,0:T(8,128)(2,1)} %param.26), channel_id=1, source_target_pairs={{0,1},{1,0},{2,3},{3,2},{4,5},{5,4},{6,7},{7,6},{8,9},{9,8},{10,11... | collective-permute-start | bytes 884744 | tf_op jit(solution)/shard_map/ppermute | solution.py:108
  1.8 36.4 %collective-permute-start.9 = (f32[768]{0:T(1024)}, f32[768]{0:T(1024)S(1)}, u32[]{:S(2)}, u32[]{:S(2)}) collective-permute-start(f32[768]{0:T(1024)} %param.28), channel_id=1, source_target_pairs={{0,1},{1,0},{2,3},{3,2},{4,5},{5,4},{6,7},{7,6},{8,9},{9,8},{10,11... | collective-permute-start | bytes 9224 | tf_op jit(solution)/shard_map/ppermute | solution.py:108
  1.8 78.4 %collective-permute-start.8 = (bf16[768,768]{1,0:T(8,128)(2,1)}, bf16[768,768]{1,0:T(8,128)(2,1)}, u32[]{:S(2)}, u32[]{:S(2)}) collective-permute-start(bf16[768,768]{1,0:T(8,128)(2,1)} %param.27), channel_id=1, source_target_pairs={{0,1},{1,0},{2,3},{3,2},{4,5},{5,4},{6,7},{7,6},{8,9},{9,8},{10,11... | collective-permute-start | bytes 3538952 | tf_op jit(solution)/shard_map/ppermute | solution.py:108
  22.5 63.1 %collective-permute-start.10 = (bf16[768,768]{1,0:T(8,128)(2,1)}, bf16[768,768]{1,0:T(8,128)(2,1)}, u32[]{:S(2)}, u32[]{:S(2)}) collective-permute-start(bf16[768,768]{1,0:T(8,128)(2,1)} %param.29), channel_id=1, source_target_pairs={{0,1},{1,0},{2,3},{3,2},{4,5},{5,4},{6,7},{7,6},{8,9},{9,8},{10,11... | collective-permute-start | bytes 3538952 | tf_op jit(solution)/shard_map/ppermute | solution.py:108
  23.4 25.2 %collective-permute-start.12 = (bf16[768,3,192]{0,2,1:T(8,128)(2,1)S(1)}, bf16[768,3,192]{0,2,1:T(8,128)(2,1)}, u32[]{:S(2)}, u32[]{:S(2)}) collective-permute-start(bf16[768,3,192]{0,2,1:T(8,128)(2,1)S(1)} %copy-done.38), channel_id=1, source_target_pairs={{0,1},{1,0},{2,3},{3,2},{4,5},{5,4},{6,7},{7,6},{8,9},{9,8},{10,11... | collective-permute-start | bytes 2654216 | tf_op jit(solution)/shard_map/ppermute | solution.py:108
  35.3 21.0 %collective-permute-start.3 = (bf16[512,768]{1,0:T(8,128)(2,1)}, bf16[512,768]{1,0:T(8,128)(2,1)}, u32[]{:S(2)}, u32[]{:S(2)}) collective-permute-start(bf16[512,768]{1,0:T(8,128)(2,1)} %convolution_convert_fusion.3), channel_id=1, source_target_pairs={{0,2},{1,3},{2,0},{3,1},{4,6},{5,7},{6,4},{7,5},{8,10},{9,11},{10,... | collective-permute-start | bytes 2359304 | tf_op jit(solution)/shard_map/ppermute | solution.py:111
  47.3 53.3 %collective-permute-start.14 = (bf16[192,768]{1,0:T(8,128)(2,1)}, bf16[192,768]{1,0:T(8,128)(2,1)}, u32[]{:S(2)}, u32[]{:S(2)}) collective-permute-start(bf16[192,768]{1,0:T(8,128)(2,1)} %param.34), channel_id=1, source_target_pairs={{0,1},{1,0},{2,3},{3,2},{4,5},{5,4},{6,7},{7,6},{8,9},{9,8},{10,11... | collective-permute-start | bytes 884744 | tf_op jit(solution)/shard_map/ppermute | solution.py:108
  51.3 57.8 %collective-permute-start.16 = (bf16[768,768]{1,0:T(8,128)(2,1)}, bf16[768,768]{1,0:T(8,128)(2,1)}, u32[]{:S(2)}, u32[]{:S(2)}) collective-permute-start(bf16[768,768]{1,0:T(8,128)(2,1)} %param.35), channel_id=1, source_target_pairs={{0,1},{1,0},{2,3},{3,2},{4,5},{5,4},{6,7},{7,6},{8,9},{9,8},{10,11... | collective-permute-start | bytes 3538952 | tf_op jit(solution)/shard_map/ppermute | solution.py:108
  73.0 6.8 %collective-permute-start.7 = (f32[32,768]{1,0:T(8,128)S(1)}, f32[32,768]{1,0:T(8,128)S(1)}, u32[]{:S(2)}, u32[]{:S(2)}) collective-permute-start(f32[32,768]{1,0:T(8,128)S(1)} %maximum_select_fusion.31), channel_id=1, source_target_pairs={{0,16},{4,20},{8,24},{12,28},{16,0},{20,4},{24,8},{28,12},{1,17},{... | collective-permute-start | bytes 294920 | tf_op jit(solution)/shard_map/ppermute | solution.py:164
  79.9 31.8 %collective-permute-start.18 = (bf16[768,768]{1,0:T(8,128)(2,1)}, bf16[768,768]{1,0:T(8,128)(2,1)}, u32[]{:S(2)}, u32[]{:S(2)}) collective-permute-start(bf16[768,768]{1,0:T(8,128)(2,1)} %param.37), channel_id=1, source_target_pairs={{0,1},{1,0},{2,3},{3,2},{4,5},{5,4},{6,7},{7,6},{8,9},{9,8},{10,11... | collective-permute-start | bytes 3538952 | tf_op jit(solution)/shard_map/ppermute | solution.py:108
  80.2 41.4 %collective-permute-start.25 = (f32[32,768]{1,0:T(8,128)}, f32[32,768]{1,0:T(8,128)}, u32[]{:S(2)}, u32[]{:S(2)}) collective-permute-start(f32[32,768]{1,0:T(8,128)} %maximum_select_fusion.32), channel_id=1, source_target_pairs={{0,16},{4,20},{8,24},{12,28},{16,0},{20,4},{24,8},{28,12},{1,17},{... | collective-permute-start | bytes 294920 | tf_op jit(solution)/shard_map/ppermute | solution.py:164
  88.1 7.1 %collective-permute-start.11 = (f32[64,768]{1,0:T(8,128)S(1)}, f32[64,768]{1,0:T(8,128)S(1)}, u32[]{:S(2)}, u32[]{:S(2)}) collective-permute-start(f32[64,768]{1,0:T(8,128)S(1)} %fusion.165), channel_id=1, source_target_pairs={{0,2},{1,3},{2,0},{3,1},{4,6},{5,7},{6,4},{7,5},{8,10},{9,11},{10,... | collective-permute-start | bytes 589832 | tf_op jit(solution)/shard_map/ppermute | solution.py:111
  95.2 229.2 %collective-permute-start.50 = (bf16[32,384]{1,0:T(8,128)(2,1)}, bf16[32,384]{1,0:T(8,128)(2,1)}, u32[]{:S(2)}, u32[]{:S(2)}) collective-permute-start(bf16[32,384]{1,0:T(8,128)(2,1)} %maximum_select_fusion.38), channel_id=1, source_target_pairs={{0,16},{4,20},{8,24},{12,28},{16,0},{20,4},{24,8},{28,12},{1,17},{... | collective-permute-start | bytes 73736 | tf_op jit(solution)/shard_map/ppermute | solution.py:164
  115.0 6.2 %collective-permute-start.19 = (f32[64,768]{1,0:T(8,128)S(1)}, f32[64,768]{1,0:T(8,128)S(1)}, u32[]{:S(2)}, u32[]{:S(2)}) collective-permute-start(f32[64,768]{1,0:T(8,128)S(1)} %fusion.35), channel_id=1, source_target_pairs={{0,2},{1,3},{2,0},{3,1},{4,6},{5,7},{6,4},{7,5},{8,10},{9,11},{10,... | collective-permute-start | bytes 589832 | tf_op jit(solution)/shard_map/ppermute | solution.py:111
  119.7 32.7 %collective-permute-start.20 = (bf16[512,768]{1,0:T(8,128)(2,1)S(1)}, bf16[512,768]{1,0:T(8,128)(2,1)S(1)}, u32[]{:S(2)}, u32[]{:S(2)}) collective-permute-start(bf16[512,768]{1,0:T(8,128)(2,1)S(1)} %convolution_convert_fusion.1), channel_id=1, source_target_pairs={{0,2},{1,3},{2,0},{3,1},{4,6},{5,7},{6,4},{7,5},{8,10},{9,11},{10,... | collective-permute-start | bytes 2359304 | tf_op jit(solution)/shard_map/ppermute | solution.py:111
  143.5 36.4 %collective-permute-start.26 = (f32[64,768]{1,0:T(8,128)}, f32[64,768]{1,0:T(8,128)}, u32[]{:S(2)}, u32[]{:S(2)}) collective-permute-start(f32[64,768]{1,0:T(8,128)} %fusion.36), channel_id=1, source_target_pairs={{0,2},{1,3},{2,0},{3,1},{4,6},{5,7},{6,4},{7,5},{8,10},{9,11},{10,... | collective-permute-start | bytes 589832 | tf_op jit(solution)/shard_map/ppermute | solution.py:111
  171.6 55.2 %collective-permute-start.29 = (bf16[512,768]{1,0:T(8,128)(2,1)}, bf16[512,768]{1,0:T(8,128)(2,1)}, u32[]{:S(2)}, u32[]{:S(2)}) collective-permute-start(bf16[512,768]{1,0:T(8,128)(2,1)} %convolution_convert_fusion), channel_id=1, source_target_pairs={{0,2},{1,3},{2,0},{3,1},{4,6},{5,7},{6,4},{7,5},{8,10},{9,11},{10,... | collective-permute-start | bytes 2359304 | tf_op jit(solution)/shard_map/ppermute | solution.py:111
  175.1 133.0 %collective-permute-start.58 = (bf16[768,768]{1,0:T(8,128)(2,1)}, bf16[768,768]{1,0:T(8,128)(2,1)}, u32[]{:S(2)}, u32[]{:S(2)}) collective-permute-start(bf16[768,768]{1,0:T(8,128)(2,1)} %dynamic-slice_convert_fusion), channel_id=1, source_target_pairs={{0,1},{1,0},{2,3},{3,2},{4,5},{5,4},{6,7},{7,6},{8,9},{9,8},{10,11... | collective-permute-start | bytes 3538952 | tf_op jit(solution)/shard_map/ppermute | solution.py:108
  177.9 140.6 %collective-permute-start.51 = (bf16[768,768]{1,0:T(8,128)(2,1)}, bf16[768,768]{1,0:T(8,128)(2,1)}, u32[]{:S(2)}, u32[]{:S(2)}) collective-permute-start(bf16[768,768]{1,0:T(8,128)(2,1)} %dynamic-slice_convert_fusion.1), channel_id=1, source_target_pairs={{0,1},{1,0},{2,3},{3,2},{4,5},{5,4},{6,7},{7,6},{8,9},{9,8},{10,11... | collective-permute-start | bytes 3538952 | tf_op jit(solution)/shard_map/ppermute | solution.py:108
  202.5 7.1 %collective-permute-start.27 = (f32[64,768]{1,0:T(8,128)S(1)}, f32[64,768]{1,0:T(8,128)S(1)}, u32[]{:S(2)}, u32[]{:S(2)}) collective-permute-start(f32[64,768]{1,0:T(8,128)S(1)} %fusion.64), channel_id=1, source_target_pairs={{0,2},{1,3},{2,0},{3,1},{4,6},{5,7},{6,4},{7,5},{8,10},{9,11},{10,... | collective-permute-start | bytes 589832 | tf_op jit(solution)/shard_map/ppermute | solution.py:111
  216.9 6.3 %collective-permute-start.28 = (f32[64,768]{1,0:T(8,128)S(1)}, f32[64,768]{1,0:T(8,128)S(1)}, u32[]{:S(2)}, u32[]{:S(2)}) collective-permute-start(f32[64,768]{1,0:T(8,128)S(1)} %fusion.166), channel_id=1, source_target_pairs={{0,2},{1,3},{2,0},{3,1},{4,6},{5,7},{6,4},{7,5},{8,10},{9,11},{10,... | collective-permute-start | bytes 589832 | tf_op jit(solution)/shard_map/ppermute | solution.py:111
  223.2 23.9 %collective-permute-start.21 = (bf16[512,768]{1,0:T(8,128)(2,1)}, bf16[512,768]{1,0:T(8,128)(2,1)}, u32[]{:S(2)}, u32[]{:S(2)}) collective-permute-start(bf16[512,768]{1,0:T(8,128)(2,1)} %fusion.11), channel_id=1, source_target_pairs={{0,1},{1,0},{2,3},{3,2},{4,5},{5,4},{6,7},{7,6},{8,9},{9,8},{10,11... | collective-permute-start | bytes 2359304 | tf_op jit(solution)/shard_map/ppermute | solution.py:108
  240.6 12.1 %collective-permute-start.39 = (f32[9,768]{1,0:T(8,128)S(1)}, f32[9,768]{1,0:T(8,128)S(1)}, u32[]{:S(2)}, u32[]{:S(2)}) collective-permute-start(f32[9,768]{1,0:T(8,128)S(1)} %concatenate.347), channel_id=1, source_target_pairs={{0,1},{1,0},{2,3},{3,2},{4,5},{5,4},{6,7},{7,6},{8,9},{9,8},{10,11... | collective-permute-start | bytes 82952 | tf_op jit(solution)/shard_map/ppermute | solution.py:108
  247.1 43.5 %collective-permute-start.40 = (bf16[192,768]{1,0:T(8,128)(2,1)S(1)}, bf16[192,768]{1,0:T(8,128)(2,1)}, u32[]{:S(2)}, u32[]{:S(2)}) collective-permute-start(bf16[192,768]{1,0:T(8,128)(2,1)S(1)} %dynamic-slice_convert_fusion.3), channel_id=1, source_target_pairs={{0,1},{1,0},{2,3},{3,2},{4,5},{5,4},{6,7},{7,6},{8,9},{9,8},{10,11... | collective-permute-start | bytes 884744 | tf_op jit(solution)/shard_map/ppermute | solution.py:108
  252.8 79.2 %collective-permute-start.32 = (bf16[768,3,192]{0,2,1:T(8,128)(2,1)}, bf16[768,3,192]{0,2,1:T(8,128)(2,1)}, u32[]{:S(2)}, u32[]{:S(2)}) collective-permute-start(bf16[768,3,192]{0,2,1:T(8,128)(2,1)} %dynamic-slice_convert_fusion.2), channel_id=1, source_target_pairs={{0,1},{1,0},{2,3},{3,2},{4,5},{5,4},{6,7},{7,6},{8,9},{9,8},{10,11... | collective-permute-start | bytes 2654216 | tf_op jit(solution)/shard_map/ppermute | solution.py:108
  306.5 16.5 %collective-permute-start.30 = (bf16[512,768]{1,0:T(8,128)(2,1)}, bf16[512,768]{1,0:T(8,128)(2,1)S(1)}, u32[]{:S(2)}, u32[]{:S(2)}) collective-permute-start(bf16[512,768]{1,0:T(8,128)(2,1)} %convolution_convert_fusion.2), channel_id=1, source_target_pairs={{0,2},{1,3},{2,0},{3,1},{4,6},{5,7},{6,4},{7,5},{8,10},{9,11},{10,... | collective-permute-start | bytes 2359304 | tf_op jit(solution)/shard_map/ppermute | solution.py:111
  318.5 15.0 %collective-permute-start.59 = (bf16[384,768]{1,0:T(8,128)(2,1)S(1)}, bf16[384,768]{1,0:T(8,128)(2,1)S(1)}, u32[]{:S(2)}, u32[]{:S(2)}) collective-permute-start(bf16[384,768]{1,0:T(8,128)(2,1)S(1)} %constant_dynamic-slice_fusion.2), channel_id=1, source_target_pairs={{0,4},{4,0},{8,12},{12,8},{16,20},{20,16},{24,28},{28,24},{1,5},{5... | collective-permute-start | bytes 1769480 | tf_op jit(solution)/shard_map/ppermute | solution.py:187
  318.6 11.4 %collective-permute-start.46 = (bf16[96,768]{1,0:T(8,128)(2,1)S(1)}, bf16[96,768]{1,0:T(8,128)(2,1)S(1)}, u32[]{:S(2)}, u32[]{:S(2)}) collective-permute-start(bf16[96,768]{1,0:T(8,128)(2,1)S(1)} %maximum_select_fusion.28), channel_id=1, source_target_pairs={{0,4},{4,0},{8,12},{12,8},{16,20},{20,16},{24,28},{28,24},{1,5},{5... | collective-permute-start | bytes 442376 | tf_op jit(solution)/shard_map/ppermute | solution.py:190
  323.0 12.8 %collective-permute-start.52 = (bf16[384,768]{1,0:T(8,128)(2,1)S(1)}, bf16[384,768]{1,0:T(8,128)(2,1)S(1)}, u32[]{:S(2)}, u32[]{:S(2)}) collective-permute-start(bf16[384,768]{1,0:T(8,128)(2,1)S(1)} %constant_dynamic-slice_fusion.5), channel_id=1, source_target_pairs={{0,8},{4,12},{8,0},{12,4},{16,24},{20,28},{24,16},{28,20},{1,9},{5... | collective-permute-start | bytes 1769480 | tf_op jit(solution)/shard_map/ppermute | solution.py:187
  324.4 79.1 %collective-permute-start.31 = (f32[512,768]{1,0:T(8,128)S(1)}, f32[512,768]{1,0:T(8,128)S(1)}, u32[]{:S(2)}, u32[]{:S(2)}) collective-permute-start(f32[512,768]{1,0:T(8,128)S(1)} %fusion.10), channel_id=1, source_target_pairs={{0,1},{1,0},{2,3},{3,2},{4,5},{5,4},{6,7},{7,6},{8,9},{9,8},{10,11... | collective-permute-start | bytes 4718600 | tf_op jit(solution)/shard_map/ppermute | solution.py:108
  333.4 19.0 %collective-permute-start.33 = (bf16[384,576]{0,1:T(8,128)(2,1)S(1)}, bf16[384,576]{0,1:T(8,128)(2,1)S(1)}, u32[]{:S(2)}, u32[]{:S(2)}) collective-permute-start(bf16[384,576]{0,1:T(8,128)(2,1)S(1)} %constant_dynamic-slice_fusion.12), channel_id=1, source_target_pairs={{0,8},{4,12},{8,0},{12,4},{16,24},{20,28},{24,16},{28,20},{1,9},{5... | collective-permute-start | bytes 1327112 | tf_op jit(solution)/shard_map/ppermute | solution.py:187
  333.7 15.4 %collective-permute-start.60 = (bf16[192,768]{1,0:T(8,128)(2,1)S(1)}, bf16[192,768]{1,0:T(8,128)(2,1)S(1)}, u32[]{:S(2)}, u32[]{:S(2)}) collective-permute-start(bf16[192,768]{1,0:T(8,128)(2,1)S(1)} %constant_dynamic-slice_fusion.1), channel_id=1, source_target_pairs={{0,8},{4,12},{8,0},{12,4},{16,24},{20,28},{24,16},{28,20},{1,9},{5... | collective-permute-start | bytes 884744 | tf_op jit(solution)/shard_map/ppermute | solution.py:187
  336.0 13.8 %collective-permute-start.53 = (bf16[192,768]{1,0:T(8,128)(2,1)S(1)}, bf16[192,768]{1,0:T(8,128)(2,1)S(1)}, u32[]{:S(2)}, u32[]{:S(2)}) collective-permute-start(bf16[192,768]{1,0:T(8,128)(2,1)S(1)} %constant_dynamic-slice_fusion.4), channel_id=1, source_target_pairs={{0,4},{4,0},{8,12},{12,8},{16,20},{20,16},{24,28},{28,24},{1,5},{5... | collective-permute-start | bytes 884744 | tf_op jit(solution)/shard_map/ppermute | solution.py:187
  349.2 15.6 %collective-permute-start.61 = (bf16[96,768]{1,0:T(8,128)(2,1)S(1)}, bf16[96,768]{1,0:T(8,128)(2,1)S(1)}, u32[]{:S(2)}, u32[]{:S(2)}) collective-permute-start(bf16[96,768]{1,0:T(8,128)(2,1)S(1)} %constant_dynamic-slice_fusion), channel_id=1, source_target_pairs={{0,16},{4,20},{8,24},{12,28},{16,0},{20,4},{24,8},{28,12},{1,17},{... | collective-permute-start | bytes 442376 | tf_op jit(solution)/shard_map/ppermute | solution.py:187
  349.9 24.4 %collective-permute-start.54 = (bf16[96,768]{1,0:T(8,128)(2,1)S(1)}, bf16[96,768]{1,0:T(8,128)(2,1)S(1)}, u32[]{:S(2)}, u32[]{:S(2)}) collective-permute-start(bf16[96,768]{1,0:T(8,128)(2,1)S(1)} %constant_dynamic-slice_fusion.3), channel_id=1, source_target_pairs={{0,16},{4,20},{8,24},{12,28},{16,0},{20,4},{24,8},{28,12},{1,17},{... | collective-permute-start | bytes 442376 | tf_op jit(solution)/shard_map/ppermute | solution.py:187
  352.7 12.2 %collective-permute-start.34 = (bf16[192,576]{0,1:T(8,128)(2,1)S(1)}, bf16[192,576]{0,1:T(8,128)(2,1)S(1)}, u32[]{:S(2)}, u32[]{:S(2)}) collective-permute-start(bf16[192,576]{0,1:T(8,128)(2,1)S(1)} %constant_dynamic-slice_fusion.11), channel_id=1, source_target_pairs={{0,4},{4,0},{8,12},{12,8},{16,20},{20,16},{24,28},{28,24},{1,5},{5... | collective-permute-start | bytes 663560 | tf_op jit(solution)/shard_map/ppermute | solution.py:187
  364.8 15.4 %collective-permute-start.62 = (bf16[96,768]{1,0:T(8,128)(2,1)S(1)}, bf16[96,768]{1,0:T(8,128)(2,1)S(1)}, u32[]{:S(2)}, u32[]{:S(2)}) collective-permute-start(bf16[96,768]{1,0:T(8,128)(2,1)S(1)} %add_convert_fusion.10), channel_id=1, source_target_pairs={{0,16},{4,20},{8,24},{12,28},{16,0},{20,4},{24,8},{28,12},{1,17},{... | collective-permute-start | bytes 442376 | tf_op jit(solution)/shard_map/ppermute | solution.py:190
  365.2 14.8 %collective-permute-start.35 = (bf16[96,576]{0,1:T(8,128)(2,1)S(1)}, bf16[96,576]{0,1:T(8,128)(2,1)S(1)}, u32[]{:S(2)}, u32[]{:S(2)}) collective-permute-start(bf16[96,576]{0,1:T(8,128)(2,1)S(1)} %constant_dynamic-slice_fusion.10), channel_id=1, source_target_pairs={{0,16},{4,20},{8,24},{12,28},{16,0},{20,4},{24,8},{28,12},{1,17},{... | collective-permute-start | bytes 331784 | tf_op jit(solution)/shard_map/ppermute | solution.py:187
  374.3 12.3 %collective-permute-start.55 = (bf16[96,768]{1,0:T(8,128)(2,1)S(1)}, bf16[96,768]{1,0:T(8,128)(2,1)S(1)}, u32[]{:S(2)}, u32[]{:S(2)}) collective-permute-start(bf16[96,768]{1,0:T(8,128)(2,1)S(1)} %add_convert_fusion.11), channel_id=1, source_target_pairs={{0,16},{4,20},{8,24},{12,28},{16,0},{20,4},{24,8},{28,12},{1,17},{... | collective-permute-start | bytes 442376 | tf_op jit(solution)/shard_map/ppermute | solution.py:190
  380.1 6.2 %collective-permute-start.36 = (bf16[96,576]{0,1:T(8,128)(2,1)S(1)}, bf16[96,576]{0,1:T(8,128)(2,1)S(1)}, u32[]{:S(2)}, u32[]{:S(2)}) collective-permute-start(bf16[96,576]{0,1:T(8,128)(2,1)S(1)} %add_convert_fusion.13), channel_id=1, source_target_pairs={{0,16},{4,20},{8,24},{12,28},{16,0},{20,4},{24,8},{28,12},{1,17},{... | collective-permute-start | bytes 331784 | tf_op jit(solution)/shard_map/ppermute | solution.py:190
  380.3 16.8 %collective-permute-start.63 = (bf16[192,768]{1,0:T(8,128)(2,1)S(1)}, bf16[192,768]{1,0:T(8,128)(2,1)S(1)}, u32[]{:S(2)}, u32[]{:S(2)}) collective-permute-start(bf16[192,768]{1,0:T(8,128)(2,1)S(1)} %maximum_select_fusion.25), channel_id=1, source_target_pairs={{0,8},{4,12},{8,0},{12,4},{16,24},{20,28},{24,16},{28,20},{1,9},{5... | collective-permute-start | bytes 884744 | tf_op jit(solution)/shard_map/ppermute | solution.py:190
  386.6 10.0 %collective-permute-start.37 = (bf16[192,576]{0,1:T(8,128)(2,1)S(1)}, bf16[192,576]{0,1:T(8,128)(2,1)S(1)}, u32[]{:S(2)}, u32[]{:S(2)}) collective-permute-start(bf16[192,576]{0,1:T(8,128)(2,1)S(1)} %maximum_select_fusion.22), channel_id=1, source_target_pairs={{0,4},{4,0},{8,12},{12,8},{16,20},{20,16},{24,28},{28,24},{1,5},{5... | collective-permute-start | bytes 663560 | tf_op jit(solution)/shard_map/ppermute | solution.py:190
  386.7 16.2 %collective-permute-start.56 = (bf16[192,768]{1,0:T(8,128)(2,1)S(1)}, bf16[192,768]{1,0:T(8,128)(2,1)S(1)}, u32[]{:S(2)}, u32[]{:S(2)}) collective-permute-start(bf16[192,768]{1,0:T(8,128)(2,1)S(1)} %maximum_select_fusion.24), channel_id=1, source_target_pairs={{0,4},{4,0},{8,12},{12,8},{16,20},{20,16},{24,28},{28,24},{1,5},{5... | collective-permute-start | bytes 884744 | tf_op jit(solution)/shard_map/ppermute | solution.py:190
  397.0 13.0 %collective-permute-start.38 = (bf16[384,576]{0,1:T(8,128)(2,1)S(1)}, bf16[384,576]{0,1:T(8,128)(2,1)S(1)}, u32[]{:S(2)}, u32[]{:S(2)}) collective-permute-start(bf16[384,576]{0,1:T(8,128)(2,1)S(1)} %maximum_select_fusion.16), channel_id=1, source_target_pairs={{0,8},{4,12},{8,0},{12,4},{16,24},{20,28},{24,16},{28,20},{1,9},{5... | collective-permute-start | bytes 1327112 | tf_op jit(solution)/shard_map/ppermute | solution.py:190
  397.2 15.5 %collective-permute-start.64 = (bf16[384,768]{1,0:T(8,128)(2,1)S(1)}, bf16[384,768]{1,0:T(8,128)(2,1)S(1)}, u32[]{:S(2)}, u32[]{:S(2)}) collective-permute-start(bf16[384,768]{1,0:T(8,128)(2,1)S(1)} %maximum_select_fusion.14), channel_id=1, source_target_pairs={{0,4},{4,0},{8,12},{12,8},{16,20},{20,16},{24,28},{28,24},{1,5},{5... | collective-permute-start | bytes 1769480 | tf_op jit(solution)/shard_map/ppermute | solution.py:190
  403.1 14.5 %collective-permute-start.57 = (bf16[384,768]{1,0:T(8,128)(2,1)S(1)}, bf16[384,768]{1,0:T(8,128)(2,1)S(1)}, u32[]{:S(2)}, u32[]{:S(2)}) collective-permute-start(bf16[384,768]{1,0:T(8,128)(2,1)S(1)} %maximum_select_fusion.13), channel_id=1, source_target_pairs={{0,8},{4,12},{8,0},{12,4},{16,24},{20,28},{24,16},{28,20},{1,9},{5... | collective-permute-start | bytes 1769480 | tf_op jit(solution)/shard_map/ppermute | solution.py:190
  (143 other events, 1079.0 us)
